TPU v7x, 128 devices: a whole 4x4x4 slice. The times are simulated.
128 devices in a mesh: seq: 64 (over z, x, y_hi, core), ch: 2 (over y_lo).
Axes of the slice: x: 4, y: 4 (y_hi: 2, y_lo: 2; y = y_hi * 2 + y_lo), z: 4, core: 2. Of those that a mesh axis runs over, the one named last changes fastest.
Arguments:
- inputs: bfloat16 [2, 65536, 1536], P(None, 'seq', 'ch'), may hold values from -6 to 6
- cotangent: bfloat16 [2, 65536, 1536], P(None, 'seq', 'ch'), may hold values from -6 to 6
- conv_out: bfloat16 [2, 65536, 768], P(None, 'seq'), may hold values from -6 to 6
- conv_weight: bfloat16 [3, 1536, 768], P(None, 'ch'), may hold values from -0.09375 to 0.09375
- proj_weight: bfloat16 [768, 1536], P(None, 'ch'), may hold values from -0.21875 to 0.21875
Outputs:
- grad_inputs: bfloat16 [2, 65536, 1536], P(None, 'seq', 'ch')
- grad_conv: bfloat16 [3, 1536, 768], P(None, 'ch')
- grad_proj: bfloat16 [768, 1536], P(None, 'ch')
All inputs are finite; a program needn't handle non-finite values.
Results may differ from a plain program's by a relative error of at most 0.0061.
Values may be sent and summed in bfloat16 or wider, within the bound.
A program may use at most 128 MiB of HBM per device.

v0:
```python
import math
import jax
import jax.numpy as jnp
from jax import lax
from jax.sharding import PartitionSpec as P

DILATION_STEP = 2048


def shifted(value, axis, steps):
    count = lax.axis_size(axis)
    leading, last = (max(0, -steps), min(count, count - steps))
    return lax.ppermute(value, axis, [(source, source + steps) for source in range(leading, last)])


def contract_rows(left, right):
    return lax.dot_general(
        left, right, (((0,), (0,)), ((), ())), preferred_element_type=jnp.float32
    )


def gelu_parts(values):
    wide = values.astype(jnp.float32)
    cumul = 0.5 * (1.0 + jax.scipy.special.erf(wide / math.sqrt(2.0)))
    dense = jnp.exp(-0.5 * wide * wide) / math.sqrt(2.0 * math.pi)
    return (wide * cumul, cumul + wide * dense)


def shards(inputs, cotangent, conv_out, conv_weight, proj_weight):
    batches, sequence_length, chan_part = inputs.shape
    inner_width = conv_out.shape[2]
    row_count = batches * sequence_length
    flat_g = cotangent.reshape(row_count, chan_part)
    partial_mid = jnp.dot(flat_g, proj_weight.T, preferred_element_type=jnp.float32)
    summed_mid = lax.psum(partial_mid, "ch")
    middle_gradient = summed_mid.astype(jnp.bfloat16).reshape(batches, sequence_length, inner_width)
    neighbor_hops = DILATION_STEP // sequence_length
    following = shifted(middle_gradient, "seq", -neighbor_hops)
    preceding = shifted(middle_gradient, "seq", neighbor_hops)
    tap_list = (
        following.reshape(row_count, inner_width),
        middle_gradient.reshape(row_count, inner_width),
        preceding.reshape(row_count, inner_width),
    )
    grad_hidden = jnp.zeros((row_count, chan_part), jnp.float32)
    for tap_index in range(3):
        grad_hidden = grad_hidden + jnp.dot(
            tap_list[tap_index], conv_weight[tap_index].T, preferred_element_type=jnp.float32
        )
    hidden_full, deriv = gelu_parts(inputs.reshape(row_count, chan_part))
    hidden = hidden_full.astype(jnp.bfloat16)
    grad_inputs = (flat_g.astype(jnp.float32) + grad_hidden * deriv).astype(jnp.bfloat16)
    grad_inputs = grad_inputs.reshape(batches, sequence_length, chan_part)
    grad_scale = 1.0 / math.sqrt(float(row_count * lax.axis_size("seq")))
    conv_terms = jnp.stack(
        [contract_rows(hidden, tap_list[tap_index]) * grad_scale for tap_index in range(3)]
    )
    proj_terms = contract_rows(conv_out.reshape(row_count, inner_width), flat_g) * grad_scale
    conv_total, proj_total = lax.psum((conv_terms, proj_terms), "seq")
    return (grad_inputs, conv_total.astype(jnp.bfloat16), proj_total.astype(jnp.bfloat16))


def solution(mesh):
    in_specs = (
        P(None, "seq", "ch"),
        P(None, "seq", "ch"),
        P(None, "seq", None),
        P(None, "ch", None),
        P(None, "ch"),
    )
    out_specs = (P(None, "seq", "ch"), P(None, "ch", None), P(None, "ch"))
    return jax.shard_map(shards, mesh=mesh, in_specs=in_specs, out_specs=out_specs, check_vma=False)
```

profile of v0, /device:TPU:0, one launch (start us, length us, event | category | flops | bytes accessed | tf_op | source)
XLA Modules:
  0.0 702.9 jit_solution(10845579516698475319)
XLA Ops:
  0.6 0.0 copy-start
  0.6 7.7 %fusion.29 = f32[2048,768]{1,0:T(8,128)} fusion(bf16[2048,768]{1,0:T(8,128)(2,1)} %bitcast.60, bf16[768,768]{1,0:T(8,128)(2,1)} %param.9), kind=kOutput, calls=%fused_computation.36 | convolution fusion | flops 2415919104 | bytes 10616832 | tf_op jit(solution)/shard_map/dot_general | solution.py:34
  8.3 148.1 %all-reduce.3 = bf16[2048,768]{1,0:T(8,128)(2,1)} all-reduce(f32[2048,768]{1,0:T(8,128)} %fusion.29), channel_id=1, replica_groups=mesh['seq'=64,'ch'=2] {'ch'}, use_global_device_ids=true, to_apply=%region_0.0 | all-reduce | flops 1572864 | bytes 9437184 | tf_op jit(solution)/shard_map/psum | solution.py:35
  156.4 0.0 copy-start.3
  156.4 0.0 copy-start.5
  156.4 1.5 collective-permute-start
  157.9 6.3 collective-permute-start.1
  164.2 0.0 copy-done
  164.2 6.0 bitcast_multiply_fusion.2
  170.2 0.0 copy-done.3
  170.2 0.0 copy-done.5
  170.2 0.0 copy-start.2
  170.2 4.8 fusion.21
  175.0 0.0 copy-done.2
  175.0 1.6 fusion.10
  176.6 4.0 fusion.14
  180.6 2.7 multiply_bitcast_fusion
  183.3 112.8 %collective-permute-done = bf16[2,1024,768]{2,1,0:T(8,128)(2,1)S(1)} collective-permute-done((bf16[2,1024,768]{2,1,0:T(8,128)(2,1)}, bf16[2,1024,768]{2,1,0:T(8,128)(2,1)S(1)}, u32[]{:S(2)}, u32[]{:S(2)}) %collective-permute-start) | collective-permute-done | bytes 3145760 | tf_op jit(solution)/shard_map/ppermute | solution.py:13
  296.1 4.5 fusion.23
  300.6 2.7 fusion.16
  303.4 0.0 collective-permute-done.1
  303.4 0.0 copy-start.4
  303.4 1.6 copy-done.4
  305.0 2.7 fusion.15
  307.7 3.4 pad_maximum_fusion
  311.1 376.2 %all-reduce.4 = (bf16[3,768,768]{2,1,0:T(8,128)(2,1)}, bf16[768,768]{1,0:T(8,128)(2,1)}) all-reduce(f32[3,768,768]{2,1,0:T(8,128)} %pad_maximum_fusion, f32[768,768]{1,0:T(8,128)} %bitcast_multiply_fusion.2), channel_id=1, replica_groups=mesh['seq'=64,'ch'=2] {'seq'}, use_global_device_ids=true, to_apply=%region_1.0 | all-reduce | flops 2359296 | bytes 14155776 | tf_op jit(solution)/shard_map/psum | solution.py:59
  687.3 0.0 copy-start.1
  687.3 15.6 %fusion.6 = bf16[2048,768]{1,0:T(8,128)(2,1)} fusion(f32[2048,768]{1,0:T(8,128)} %get-tuple-element.6, bf16[2,1024,768]{2,1,0:T(8,128)(2,1)} %param.5, f32[2048,768]{1,0:T(8,128)} %fusion.23, f32[2048,768]{1,0:T(8,128)} %fusion.21, bf16[2048,768]{1,0:T(8,128)(2,1)} %bitcast.61, bf16[2048,768]{1,0:T(8,128)(2,1)} %bitcast.62, bf16[3,768,768]{2,1,0:T(8,128)(2,1)} %param.8), kind=kOutput, calls=%fused_computation.8 | convolution fusion | flops 2434793472 | bytes 32636928 | tf_op jit(solution)/shard_map/dot_general | solution.py:47
  702.9 0.0 copy-done.1
Async XLA Ops:
  0.6 163.6 %copy-start = (bf16[2,1024,768]{2,1,0:T(8,128)(2,1)S(1)}, bf16[2,1024,768]{2,1,0:T(8,128)(2,1)}, u32[]{:S(2)}) copy-start(bf16[2,1024,768]{2,1,0:T(8,128)(2,1)} %param.7) | copy-start | bytes 9437188
  156.4 13.8 %copy-start.3 = (bf16[2048,768]{1,0:T(8,128)(2,1)S(1)}, bf16[2048,768]{1,0:T(8,128)(2,1)}, u32[]{:S(2)}) copy-start(bf16[2048,768]{1,0:T(8,128)(2,1)} %all-reduce.3) | copy-start | bytes 9437188
  156.4 13.8 %copy-start.5 = (bf16[3,768,768]{2,1,0:T(8,128)(2,1)S(1)}, bf16[3,768,768]{2,1,0:T(8,128)(2,1)}, u32[]{:S(2)}) copy-start(bf16[3,768,768]{2,1,0:T(8,128)(2,1)} %param.8) | copy-start | bytes 10616836
  156.4 139.7 %collective-permute-start = (bf16[2,1024,768]{2,1,0:T(8,128)(2,1)}, bf16[2,1024,768]{2,1,0:T(8,128)(2,1)S(1)}, u32[]{:S(2)}, u32[]{:S(2)}) collective-permute-start(bf16[2,1024,768]{2,1,0:T(8,128)(2,1)} %bitcast.58), channel_id=1, source_target_pairs={{4,0},{6,2},{8,4},{10,6},{12,8},{14,10},{16,12},{18,14},{20,16},{2... | collective-permute-start | bytes 9437192 | tf_op jit(solution)/shard_map/ppermute | solution.py:13
  157.9 145.4 %collective-permute-start.1 = (bf16[2,1024,768]{2,1,0:T(8,128)(2,1)}, bf16[2,1024,768]{2,1,0:T(8,128)(2,1)S(1)}, u32[]{:S(2)}, u32[]{:S(2)}) collective-permute-start(bf16[2,1024,768]{2,1,0:T(8,128)(2,1)} %bitcast.59), channel_id=1, source_target_pairs={{0,4},{2,6},{4,8},{6,10},{8,12},{10,14},{12,16},{14,18},{16,20},{1... | collective-permute-start | bytes 9437192 | tf_op jit(solution)/shard_map/ppermute | solution.py:13
  170.2 4.8 copy-start.2
  303.4 1.6 copy-start.4
  687.3 15.6 %copy-start.1 = (bf16[2,1024,768]{2,1,0:T(8,128)(2,1)S(1)}, bf16[2,1024,768]{2,1,0:T(8,128)(2,1)}, u32[]{:S(2)}) copy-start(bf16[2,1024,768]{2,1,0:T(8,128)(2,1)} %param.7) | copy-start | bytes 9437188
where the time goes:
time: 703 us
  blocking collectives  524 us (75%)
  waiting for transfers between devices  113 us (16%)
  matrix products  46.7 us (7%)
  other arithmetic  8.96 us (1%)
  starting transfers between devices  7.8 us (1%)
    psum x1, blocking collectives, shards(): conv_total, proj_total = lax.psum((conv_terms, proj_terms), 'seq')  376 us
    psum x1, blocking collectives, shards(): summed_mid = lax.psum(partial_mid, 'ch')  148 us
    ppermute x2, waiting for transfers between devices, shifted(): lax.ppermute(value, axis, [(source, source + steps) for source in range(l...  113 us
    dot_general x3, matrix products, shards(): jnp.dot(tap_list[tap_index], conv_weight[tap_index].T, preferred_element_...  24.8 us
    dot_general x4, matrix products, contract_rows(): lax.dot_general(left, right, (((0,), (0,)), ((), ())), preferred_element_...  14.2 us
  transfers between devices with their start and end apart: 2, of which 1 were waited for; matrix products, arithmetic and copies ran while one was open for 4% of the time, Pallas kernels for 0%

commit v1 on v0

--- a/solution.py
+++ b/solution.py
@@ -3,6 +3,7 @@
 import jax.numpy as jnp
 from jax import lax
 from jax.sharding import PartitionSpec as P
+from jax.lax import all_gather
 
 DILATION_STEP = 2048
 
@@ -32,7 +33,7 @@
     row_count = batches * sequence_length
     flat_g = cotangent.reshape(row_count, chan_part)
     partial_mid = jnp.dot(flat_g, proj_weight.T, preferred_element_type=jnp.float32)
-    summed_mid = lax.psum(partial_mid, "ch")
+    summed_mid = all_gather(partial_mid, "ch").sum(axis=0)
     middle_gradient = summed_mid.astype(jnp.bfloat16).reshape(batches, sequence_length, inner_width)
     neighbor_hops = DILATION_STEP // sequence_length
     following = shifted(middle_gradient, "seq", -neighbor_hops)

time: 703 us -> 736 us (1.047)
  waiting for transfers between devices: 113 us -> 271 us
  blocking collectives: 524 us -> 376 us
  between operations: 0.72 us -> 14.1 us
  other arithmetic: 8.96 us -> 19.3 us
    all_gather x0 -> x1, waiting for transfers between devices: none -> 158 us  [shards(): summed_mid = all_gather(partial_mid, 'ch').sum(axis=0)]
    psum x1 -> x0, blocking collectives: 148 us -> none  [shards(): summed_mid = lax.psum(partial_mid, 'ch')]
    reduce_sum x0 -> x1, other arithmetic: none -> 8.12 us  [shards(): summed_mid = all_gather(partial_mid, 'ch').sum(axis=0)]
  transfers between devices with their start and end apart: 2 -> 3, of which waited for: 1 -> 2; matrix products, arithmetic and copies ran while one was open for 4% -> 4% of each run, Pallas kernels for 0% -> 0%
where the time goes in v1:
time: 736 us; the launch traced here: 735 us
  blocking collectives  376 us (51%)
  waiting for transfers between devices  271 us (37%)
  matrix products  44.5 us (6%)
  other arithmetic  19.3 us (3%)
  between operations  14.1 us (2%)
  starting transfers between devices  7.78 us (1%)
    psum x1, blocking collectives, shards(): conv_total, proj_total = lax.psum((conv_terms, proj_terms), 'seq')  376 us
    all_gather x1, waiting for transfers between devices, shards(): summed_mid = all_gather(partial_mid, 'ch').sum(axis=0)  158 us
    ppermute x2, waiting for transfers between devices, shifted(): lax.ppermute(value, axis, [(source, source + steps) for source in range(l...  114 us
    dot_general x3, matrix products, shards(): jnp.dot(tap_list[tap_index], conv_weight[tap_index].T, preferred_element_...  24.6 us
  transfers between devices with their start and end apart: 3, of which 2 were waited for; matrix products, arithmetic and copies ran while one was open for 4% of the time, Pallas kernels for 0%

profile of v1, /device:TPU:0, one launch (start us, length us, event | category | flops | bytes accessed | tf_op | source)
XLA Modules:
  0.0 735.2 jit_solution(5325436519013255405)
XLA Ops:
  7.2 0.0 copy-start
  7.2 0.0 all-gather.3.cloned.1.call-start
  7.2 7.6 %fusion.29 = f32[2048,768]{1,0:T(8,128)} fusion(bf16[2048,768]{1,0:T(8,128)(2,1)} %bitcast.62, bf16[768,768]{1,0:T(8,128)(2,1)} %param.9), kind=kOutput, calls=%fused_computation.36 | convolution fusion | flops 2415919104 | bytes 10616832 | tf_op jit(solution)/shard_map/dot_general | solution.py:35
  14.8 0.0 all-gather.3.cloned.1.call-update
  14.9 157.7 %all-gather.3.cloned.1.call-done = f32[4096,768]{1,0:T(8,128)} async-done(((f32[2048,768]{1,0:T(8,128)}), f32[4096,768]{1,0:T(8,128)}) %all-gather.3.cloned.1.call-update) | async-done | bytes 12582928 | tf_op jit(solution)/shard_map/all_gather | solution.py:36
  172.5 8.1 %reduce_sum.9 = bf16[2048,768]{1,0:T(8,128)(2,1)} reduce(f32[2,2048,768]{2,1,0:T(8,128)} %bitcast.59, f32[]{:T(128)} %constant.2.clone.1), dimensions={0}, to_apply=%region_0.0 | reduce | flops 1572864 | bytes 15728644 | tf_op jit(solution)/shard_map/reduce_sum | solution.py:36
  180.7 0.0 copy-start.3
  180.7 1.5 collective-permute-start
  182.2 6.1 fusion.14
  188.4 0.0 copy-done.3
  188.4 6.2 collective-permute-start.1
  194.6 0.0 copy-done
  194.6 0.0 copy-done.4
  194.6 4.1 bitcast_multiply_fusion.2
  198.7 0.0 copy-done.2
  198.7 1.6 fusion.10
  200.4 0.4 copy-done.7
  200.7 4.5 fusion.21
  205.2 2.7 multiply_bitcast_fusion
  208.0 113.8 %collective-permute-done = bf16[2,1024,768]{2,1,0:T(8,128)(2,1)S(1)} collective-permute-done((bf16[2,1024,768]{2,1,0:T(8,128)(2,1)}, bf16[2,1024,768]{2,1,0:T(8,128)(2,1)S(1)}, u32[]{:S(2)}, u32[]{:S(2)}) %collective-permute-start) | collective-permute-done | bytes 3145760 | tf_op jit(solution)/shard_map/ppermute | solution.py:14
  321.8 4.5 fusion.23
  326.3 2.7 fusion.16
  329.0 0.0 collective-permute-done.1
  329.0 0.0 copy-start.5
  329.0 1.6 copy-done.5
  330.7 2.7 fusion.15
  333.4 0.0 copy-start.6
  333.4 3.4 pad_maximum_fusion
  336.8 0.0 copy-done.6
  336.8 376.0 %all-reduce.2 = (bf16[3,768,768]{2,1,0:T(8,128)(2,1)}, bf16[768,768]{1,0:T(8,128)(2,1)}) all-reduce(f32[3,768,768]{2,1,0:T(8,128)} %pad_maximum_fusion, f32[768,768]{1,0:T(8,128)S(1)} %copy-done.6), channel_id=1, replica_groups=mesh['seq'=64,'ch'=2] {'seq'}, use_global_device_ids=true, to_apply=%region_1.0 | all-reduce | flops 2359296 | bytes 14155776 | tf_op jit(solution)/shard_map/psum | solution.py:60
  712.8 15.6 %fusion.6 = bf16[2048,768]{1,0:T(8,128)(2,1)} fusion(f32[2048,768]{1,0:T(8,128)} %get-tuple-element.6, bf16[2,1024,768]{2,1,0:T(8,128)(2,1)} %param.5, f32[2048,768]{1,0:T(8,128)} %fusion.23, f32[2048,768]{1,0:T(8,128)} %fusion.21, bf16[2048,768]{1,0:T(8,128)(2,1)} %bitcast.63, bf16[2048,768]{1,0:T(8,128)(2,1)} %bitcast.64, bf16[3,768,768]{2,1,0:T(8,128)(2,1)} %param.8), kind=kOutput, calls=%fused_computation.8 | convolution fusion | flops 2434793472 | bytes 32636928 | tf_op jit(solution)/shard_map/dot_general | solution.py:48
  728.4 0.0 copy-done.1
  (4 shorter events, 0.0 us)
Async XLA Ops:
  7.2 187.4 %copy-start = (bf16[2,1024,768]{2,1,0:T(8,128)(2,1)S(1)}, bf16[2,1024,768]{2,1,0:T(8,128)(2,1)}, u32[]{:S(2)}) copy-start(bf16[2,1024,768]{2,1,0:T(8,128)(2,1)} %param.7) | copy-start | bytes 9437188
  7.2 165.4 %all-gather.3.cloned.1.call-start = ((), (), s32[]{:S(2)}) async-start(), calls=%async_computation | async-start | bytes 18874368 | tf_op jit(solution)/shard_map/all_gather | solution.py:36
  180.7 7.7 %copy-start.3 = (bf16[2048,768]{1,0:T(8,128)(2,1)S(1)}, bf16[2048,768]{1,0:T(8,128)(2,1)}, u32[]{:S(2)}) copy-start(bf16[2048,768]{1,0:T(8,128)(2,1)} %reduce_sum.9) | copy-start | bytes 9437188
  180.7 13.9 %copy-start.4 = (bf16[2,1024,768]{2,1,0:T(8,128)(2,1)S(1)}, bf16[2,1024,768]{2,1,0:T(8,128)(2,1)}, u32[]{:S(2)}) copy-start(bf16[2,1024,768]{2,1,0:T(8,128)(2,1)} %param.6) | copy-start | bytes 9437188
  180.7 141.1 %collective-permute-start = (bf16[2,1024,768]{2,1,0:T(8,128)(2,1)}, bf16[2,1024,768]{2,1,0:T(8,128)(2,1)S(1)}, u32[]{:S(2)}, u32[]{:S(2)}) collective-permute-start(bf16[2,1024,768]{2,1,0:T(8,128)(2,1)} %bitcast.60), channel_id=1, source_target_pairs={{4,0},{6,2},{8,4},{10,6},{12,8},{14,10},{16,12},{18,14},{20,16},{2... | collective-permute-start | bytes 9437192 | tf_op jit(solution)/shard_map/ppermute | solution.py:14
  188.4 10.3 %copy-start.2 = (bf16[2,1024,768]{2,1,0:T(8,128)(2,1)S(1)}, bf16[2,1024,768]{2,1,0:T(8,128)(2,1)}, u32[]{:S(2)}) copy-start(bf16[2,1024,768]{2,1,0:T(8,128)(2,1)} %param.5) | copy-start | bytes 9437188
  188.4 140.7 %collective-permute-start.1 = (bf16[2,1024,768]{2,1,0:T(8,128)(2,1)S(1)}, bf16[2,1024,768]{2,1,0:T(8,128)(2,1)S(1)}, u32[]{:S(2)}, u32[]{:S(2)}) collective-permute-start(bf16[2,1024,768]{2,1,0:T(8,128)(2,1)S(1)} %bitcast.61), channel_id=1, source_target_pairs={{0,4},{2,6},{4,8},{6,10},{8,12},{10,14},{12,16},{14,18},{16,20},{1... | collective-permute-start | bytes 9437192 | tf_op jit(solution)/shard_map/ppermute | solution.py:14
  198.7 2.0 copy-start.7
  329.0 1.6 copy-start.5
  333.4 3.4 copy-start.6
  712.8 15.6 %copy-start.1 = (bf16[2,1024,768]{2,1,0:T(8,128)(2,1)S(1)}, bf16[2,1024,768]{2,1,0:T(8,128)(2,1)}, u32[]{:S(2)}) copy-start(bf16[2,1024,768]{2,1,0:T(8,128)(2,1)} %param.7) | copy-start | bytes 9437188
Sparse Core Ops, SparseCore 0:
  15.0 157.5 all-gather.2
